TPU v7x, 32 devices: a whole 2x2x4 slice. The times are simulated.
32 devices in a mesh: rows: 4 (over y, x), cols: 8 (over z, core).
Axes of the slice: x: 2, y: 2, z: 4, core: 2. Of those that a mesh axis runs over, the one named last changes fastest.
Arguments:
- counts: bfloat16 [2048, 65536], P('rows', 'cols'), may hold values from 0 to 12, as said below
- start_a: float32 [2048, 128], P(('rows', 'cols')), may hold values from -0.4 to 0.4
- start_b: float32 [4096, 128], P(('cols', 'rows')), may hold values from -0.4 to 0.4
- start_c: float32 [16, 128], replicated, may hold values from -0.4 to 0.4
Outputs:
- factor_a: float32 [2048, 128], P(('rows', 'cols'))
- factor_b: float32 [4096, 128], P(('cols', 'rows'))
- factor_c: float32 [16, 128], replicated
Inputs may be any that keep to these rules, and one draw needn't show every extreme that they name: counts holds whole numbers.
All inputs are finite; a program needn't handle non-finite values.
Results may differ from a plain program's by a relative error of at most 0.009.
Values may be sent and summed in bfloat16 or wider, within the bound.
A program may use at most 128 MiB of HBM per device.

v0:
```python
import functools
import math

import jax
import jax.numpy as jnp
from jax import lax
from jax.experimental import pallas as pl
from jax.experimental.pallas import tpu as pltpu
from jax.sharding import PartitionSpec as P

ITERS = 2
MESH = pl.DeviceIdType.MESH
F32 = jnp.float32
BF16 = jnp.bfloat16


def kernel(nr, nc, tile, rates, counts_hbm, a_in, b_in, c_in, a_out, b_out, c_out,
           counts, all_a, all_b, send_a, send_b, recv_a, recv_b, part_c, sum_c,
           held_a, trans_a, acc_a, acc_c, resid, scaled, mixed_t, grad_b,
           cnt_sem, ag_send, ag_recv, bg_send, bg_recv, ar_send, ar_recv, br_send, br_recv,
           c1_send, c1_recv, c2_send, c2_recv):
    row, col = lax.axis_index("rows"), lax.axis_index("cols")
    rate_a, rate_b, rate_c = rates
    own_a, rank = a_in.shape
    own_b = b_in.shape[0]
    depth = c_in.shape[0]
    tiles = counts.shape[1]
    per = tiles // nr
    width = tile // depth

    half = nc // 2
    near, spot = lax.div(col, half), lax.rem(col, half)
    near_peers = [near * half + lax.rem(spot + off, half) for off in range(1, half)]
    far_peers = [(1 - near) * half + lax.rem(spot + off, half) for off in range(half)]
    col_peers = near_peers + far_peers
    row_peers = [lax.rem(row + off, nr) for off in range(1, nr)]
    half_rows = half * own_a

    def load(h, t):
        return pltpu.make_async_copy(
            counts_hbm.at[pl.ds(pl.multiple_of(h * half_rows, half_rows), half_rows),
                          pl.ds(pl.multiple_of(t * tile, tile), tile)],
            counts.at[h, t], cnt_sem.at[h, t])

    def chunk(side, d):
        return lax.rem(row + side + d, nr)

    sides = (near, 1 - near)
    for side in range(2):
        for d in range(nr):
            for s in range(per):
                load(sides[side], chunk(side, d) * per + s).start()

    all_a[0, col] = a_in[...].astype(BF16)
    all_b[0, row] = b_in[...].astype(BF16)

    barrier = pltpu.get_barrier_semaphore()
    for p in col_peers:
        pl.semaphore_signal(barrier, inc=1, device_id={"cols": p}, device_id_type=MESH)
    for p in row_peers:
        pl.semaphore_signal(barrier, inc=1, device_id={"rows": p}, device_id_type=MESH)
    pl.semaphore_wait(barrier, nc + nr - 2)

    class Exchange:
        def __init__(self, send, recv, ss, rs, axis, me):
            self.args = (send, recv, ss, rs, axis, me)

        def to(self, p):
            send, recv, ss, rs, axis, me = self.args
            return pltpu.make_async_remote_copy(
                src_ref=recv.at[me] if send is None else send.at[p], dst_ref=recv.at[me],
                send_sem=ss.at[p], recv_sem=rs.at[me], device_id={axis: p}, device_id_type=MESH)

        def start(self, peers):
            for p in peers:
                self.to(p).start()

        def wait_recv(self, peers):
            send, recv, ss, rs, axis, me = self.args
            for p in peers:
                pltpu.make_async_remote_copy(
                    src_ref=recv.at[p], dst_ref=recv.at[p], send_sem=ss.at[p], recv_sem=rs.at[p],
                    device_id={axis: p}, device_id_type=MESH).wait_recv()

        def wait_send(self, peers):
            for p in peers:
                self.to(p).wait_send()

    pending = []
    local_a, local_b, shared_c = a_in[...], b_in[...], c_in[...]

    def gather(it):
        return (Exchange(None, all_a.at[it], ag_send.at[it], ag_recv.at[it], "cols", col),
                Exchange(None, all_b.at[it], bg_send.at[it], bg_recv.at[it], "rows", row))

    gather_a, gather_b = gather(0)
    gather_b.start(row_peers)
    gather_a.start(col_peers)

    for it in range(ITERS):
        pending += [(gather_a, col_peers), (gather_b, row_peers)]
        scatter_a = Exchange(send_a.at[it], recv_a.at[it], ar_send.at[it], ar_recv.at[it], "cols", col)
        scatter_b = Exchange(send_b.at[it], recv_b.at[it], br_send.at[it], br_recv.at[it], "rows", row)
        cols_c = Exchange(None, part_c.at[it], c1_send.at[it], c1_recv.at[it], "cols", col)
        rows_c = Exchange(None, sum_c.at[it], c2_send.at[it], c2_recv.at[it], "rows", row)
        pending += [(scatter_a, col_peers), (scatter_b, row_peers), (cols_c, col_peers), (rows_c, row_peers)]
        acc_a[...] = jnp.zeros_like(acc_a)
        acc_c[...] = jnp.zeros_like(acc_c)

        for side in range(2):
            h = sides[side]
            gather_a.wait_recv((near_peers, far_peers)[side])
            rows_a = all_a[it, pl.ds(h * half, half)].reshape(half_rows, rank)
            held_a[...] = rows_a
            trans_a[...] = rows_a.T

            def produce(q, s, slot):
                t = q * per + s
                if side == 0:
                    rows_b = all_b[it, q, pl.ds(s * width, width), :].astype(F32)
                    scaled[t] = (rows_b[:, None, :] * shared_c[None, :, :]).astype(BF16).reshape(tile, rank)
                log_rate = lax.dot_general(
                    held_a[...], scaled[t], (((1,), (1,)), ((), ())), preferred_element_type=F32)
                resid[slot] = (jnp.exp(log_rate) - counts[h, t].astype(F32)).astype(BF16)

            def consume(q, s, slot):
                t = q * per + s
                acc_a[h] += jnp.dot(resid[slot], scaled[t], preferred_element_type=F32)
                turned = jnp.dot(trans_a[...], resid[slot], preferred_element_type=F32)
                if side == 0:
                    mixed_t[t] = turned
                    return
                mixed = (mixed_t[t] + turned).T.reshape(width, depth, rank)
                rows_b = all_b[it, q, pl.ds(s * width, width), :].astype(F32)
                grad_b[pl.ds(s * width, width), :] = jnp.sum(mixed * shared_c[None, :, :], axis=1)
                acc_c[...] += jnp.sum(mixed * rows_b[:, None, :], axis=0)

            def ready(d):
                q = chunk(side, d)
                if it == 0:
                    for s in range(per):
                        load(h, q * per + s).wait()
                return q

            def step(d, carry):
                q, q_next = chunk(side, d), chunk(side, d + 1)
                if side == 0 or it == 0:
                    @pl.when(d < nr - 1)
                    def _():
                        ready(d + 1)
                        if side == 0:
                            gather_b.wait_recv([q_next])
                for s in range(per):
                    if s + 1 < per:
                        produce(q, s + 1, (s + 1) % 2)
                    else:
                        produce(q_next, 0, 0)
                    consume(q, s, s % 2)
                if side == 1:
                    send_b[it, q] = grad_b[...].astype(BF16)

                    @pl.when(d < nr - 1)
                    def _():
                        scatter_b.start([q])

                return carry

            produce(ready(0), 0, 0)
            lax.fori_loop(0, nr, step, 0)

            if side == 1:
                part_c[it, col] = acc_c[...].astype(BF16)
                cols_c.start(far_peers + near_peers)
            for k in range(half):
                send_a[it, h * half + k] = acc_a[h, pl.ds(k * own_a, own_a), :].astype(BF16)
            scatter_a.start((near_peers, far_peers)[side])

        last = it == ITERS - 1
        if not last:
            gather_a, gather_b = gather(it + 1)

        scatter_b.wait_recv(row_peers)
        recv_b[it, row] = jnp.zeros((own_b, rank), BF16)
        total_b = grad_b[...] + jnp.sum(recv_b[it].astype(F32), axis=0)
        local_b = local_b - rate_b * total_b
        if last:
            b_out[...] = local_b
        else:
            all_b[it + 1, row] = local_b.astype(BF16)
            gather_b.start(row_peers)

        cols_c.wait_recv(col_peers)
        sum_c[it, row] = jnp.sum(part_c[it].astype(F32), axis=0)
        rows_c.start(row_peers)

        scatter_a.wait_recv(col_peers)
        recv_a[it, col] = jnp.zeros((own_a, rank), BF16)
        total_a = acc_a[near, pl.ds(pl.multiple_of(spot * own_a, own_a), own_a), :] + jnp.sum(recv_a[it].astype(F32), axis=0)
        local_a = local_a - rate_a * total_a
        if last:
            a_out[...] = local_a
        else:
            all_a[it + 1, col] = local_a.astype(BF16)
            gather_a.start(col_peers)

        rows_c.wait_recv(row_peers)
        shared_c = shared_c - rate_c * jnp.sum(sum_c[it], axis=0)
        if last:
            c_out[...] = shared_c

    for group, peers in pending:
        group.wait_send(peers)


def finish(a, b, c, a_out, b_out, c_out):
    a_out[...] = a[...]
    b_out[...] = b[...]
    c_out[...] = c[...]


def local(nr, nc, counts, start_a, start_b, start_c):
    rows_here, flat_width = counts.shape
    own_a, rank = start_a.shape
    own_b = start_b.shape[0]
    depth = start_c.shape[0]
    cols_here = flat_width // depth
    total_i, total_j = rows_here * nr, cols_here * nc
    rates = (0.3 / math.sqrt(total_j * depth), 0.3 / math.sqrt(total_i * depth), 0.3 / math.sqrt(total_i * total_j))
    tile = 512
    tiles = flat_width // tile
    vmem = pl.BlockSpec(memory_space=pltpu.VMEM)
    dma = pltpu.SemaphoreType.DMA
    outs = [jax.ShapeDtypeStruct(x.shape, F32) for x in (start_a, start_b, start_c)]
    half_rows = rows_here // 2
    found = pl.pallas_call(
        functools.partial(kernel, nr, nc, tile, rates),
        out_shape=outs,
        in_specs=[pl.BlockSpec(memory_space=pl.ANY), vmem, vmem, vmem],
        out_specs=[vmem] * 3,
        scratch_shapes=[
            pltpu.VMEM((2, tiles, half_rows, tile), BF16),
            pltpu.VMEM((ITERS, nc, own_a, rank), BF16),
            pltpu.VMEM((ITERS, nr, own_b, rank), BF16),
            pltpu.VMEM((ITERS, nc, own_a, rank), BF16),
            pltpu.VMEM((ITERS, nr, own_b, rank), BF16),
            pltpu.VMEM((ITERS, nc, own_a, rank), BF16),
            pltpu.VMEM((ITERS, nr, own_b, rank), BF16),
            pltpu.VMEM((ITERS, nc, depth, rank), BF16),
            pltpu.VMEM((ITERS, nr, depth, rank), F32),
            pltpu.VMEM((half_rows, rank), BF16),
            pltpu.VMEM((rank, half_rows), BF16),
            pltpu.VMEM((2, half_rows, rank), F32),
            pltpu.VMEM((depth, rank), F32),
            pltpu.VMEM((2, half_rows, tile), BF16),
            pltpu.VMEM((tiles, tile, rank), BF16),
            pltpu.VMEM((tiles, rank, tile), F32),
            pltpu.VMEM((own_b, rank), F32),
            dma((2, tiles)),
            dma((ITERS, nc)), dma((ITERS, nc)), dma((ITERS, nr)), dma((ITERS, nr)),
            dma((ITERS, nc)), dma((ITERS, nc)), dma((ITERS, nr)), dma((ITERS, nr)),
            dma((ITERS, nc)), dma((ITERS, nc)), dma((ITERS, nr)), dma((ITERS, nr)),
        ],
        compiler_params=pltpu.CompilerParams(
            collective_id=0, has_side_effects=True, vmem_limit_bytes=56 * 1024 * 1024),
    )(counts, start_a, start_b, start_c)
    return pl.pallas_call(finish, out_shape=outs, in_specs=[vmem] * 3, out_specs=[vmem] * 3)(*found)


def solution(mesh):
    nr, nc = mesh.shape["rows"], mesh.shape["cols"]
    placed = (P("rows", "cols"), P(("rows", "cols"), None), P(("cols", "rows"), None), P())
    return jax.shard_map(
        functools.partial(local, nr, nc),
        mesh=mesh,
        in_specs=placed,
        out_specs=(P(("rows", "cols"), None), P(("cols", "rows"), None), P()),
        check_vma=False,
    )
```

profile of v0, /device:TPU:0, one launch (start us, length us, event | category | flops | bytes accessed | tf_op | source)
XLA Modules:
  0.0 47.1 jit_solution(14708395882753198049)
XLA Ops:
  0.6 45.0 %shard_map.67 = (f32[64,128]{1,0:T(8,128)}, f32[128,128]{1,0:T(8,128)}, f32[16,128]{1,0:T(8,128)}) custom-call(bf16[512,8192]{1,0:T(8,128)(2,1)} %counts_hbm.1, f32[64,128]{1,0:T(8,128)} %a_in.1, f32[128,128]{1,0:T(8,128)} %b_in.1, f32[16,128]{1,0:T(8,128)} %c_in.1), custom_call_target="tpu_custom_call" | custom-call | tf_op jit(solution)/shard_map/pallas_call | solution.py:235
  45.6 1.5 %shard_map.68 = (f32[64,128]{1,0:T(8,128)}, f32[128,128]{1,0:T(8,128)}, f32[16,128]{1,0:T(8,128)}) custom-call(f32[64,128]{1,0:T(8,128)} %get-tuple-element.6.a, f32[128,128]{1,0:T(8,128)} %get-tuple-element.7.b, f32[16,128]{1,0:T(8,128)} %get-tuple-element.8.c), custom_call_target="tpu_custom_call" | custom-call | tf_op jit(solution)/shard_map/pallas_call | solution.py:266
where the time goes:
time: 47.3 us; the launch traced here: 47.1 us
  Pallas kernels  46.5 us (98%)
  between operations  0.64 us (1%)
    pallas_call x1, Pallas kernels, local(): pl.pallas_call(functools.partial(kernel, nr, nc, tile, rates), out_shape=...  45 us
    pallas_call x1, Pallas kernels, local(): pl.pallas_call(finish, out_shape=outs, in_specs=[vmem] * 3, out_specs=[vm...  1.48 us

commit v1 on v0

--- a/solution.py
+++ b/solution.py
@@ -14,8 +14,8 @@
 BF16 = jnp.bfloat16
 
 
-def kernel(nr, nc, tile, rates, counts_hbm, a_in, b_in, c_in, a_out, b_out, c_out,
-           counts, all_a, all_b, send_a, send_b, recv_a, recv_b, part_c, sum_c,
+def kernel(nr, nc, tile, rates, counts_hbm, a_hbm, b_hbm, c_hbm, a_out, b_out, c_out,
+           a_in, b_in, c_in, in_sem, counts, all_a, all_b, send_a, send_b, recv_a, recv_b, part_c, sum_c,
            held_a, trans_a, acc_a, acc_c, resid, scaled, mixed_t, grad_b,
            cnt_sem, ag_send, ag_recv, bg_send, bg_recv, ar_send, ar_recv, br_send, br_recv,
            c1_send, c1_recv, c2_send, c2_recv):
@@ -45,20 +45,28 @@
     def chunk(side, d):
         return lax.rem(row + side + d, nr)
 
+    barrier = pltpu.get_barrier_semaphore()
+    for p in col_peers:
+        pl.semaphore_signal(barrier, inc=1, device_id={"cols": p}, device_id_type=MESH)
+    for p in row_peers:
+        pl.semaphore_signal(barrier, inc=1, device_id={"rows": p}, device_id_type=MESH)
+
+    fetches = [pltpu.make_async_copy(src, dst, in_sem.at[n])
+               for n, (src, dst) in enumerate(((a_hbm, a_in), (b_hbm, b_in), (c_hbm, c_in)))]
+    for fetch in fetches:
+        fetch.start()
+
     sides = (near, 1 - near)
     for side in range(2):
         for d in range(nr):
             for s in range(per):
                 load(sides[side], chunk(side, d) * per + s).start()
 
+    for fetch in fetches:
+        fetch.wait()
     all_a[0, col] = a_in[...].astype(BF16)
     all_b[0, row] = b_in[...].astype(BF16)
 
-    barrier = pltpu.get_barrier_semaphore()
-    for p in col_peers:
-        pl.semaphore_signal(barrier, inc=1, device_id={"cols": p}, device_id_type=MESH)
-    for p in row_peers:
-        pl.semaphore_signal(barrier, inc=1, device_id={"rows": p}, device_id_type=MESH)
     pl.semaphore_wait(barrier, nc + nr - 2)
 
     class Exchange:
@@ -234,10 +242,12 @@
     half_rows = rows_here // 2
     found = pl.pallas_call(
         functools.partial(kernel, nr, nc, tile, rates),
-        out_shape=outs,
-        in_specs=[pl.BlockSpec(memory_space=pl.ANY), vmem, vmem, vmem],
+        out_shape=[pltpu.VMEM(x.shape, F32) for x in (start_a, start_b, start_c)],
+        in_specs=[pl.BlockSpec(memory_space=pl.ANY)] * 4,
         out_specs=[vmem] * 3,
         scratch_shapes=[
+            pltpu.VMEM(start_a.shape, F32), pltpu.VMEM(start_b.shape, F32), pltpu.VMEM(start_c.shape, F32),
+            dma((3,)),
             pltpu.VMEM((2, tiles, half_rows, tile), BF16),
             pltpu.VMEM((ITERS, nc, own_a, rank), BF16),
             pltpu.VMEM((ITERS, nr, own_b, rank), BF16),
@@ -263,7 +273,8 @@
         compiler_params=pltpu.CompilerParams(
             collective_id=0, has_side_effects=True, vmem_limit_bytes=56 * 1024 * 1024),
     )(counts, start_a, start_b, start_c)
-    return pl.pallas_call(finish, out_shape=outs, in_specs=[vmem] * 3, out_specs=[vmem] * 3)(*found)
+    held = [pltpu.with_memory_space_constraint(x, pltpu.VMEM) for x in found]
+    return pl.pallas_call(finish, out_shape=outs, in_specs=[vmem] * 3, out_specs=[vmem] * 3)(*held)
 
 
 def solution(mesh):

time: 47.3 us -> 45.4 us (0.960)
  Pallas kernels: 46.5 us -> 44.6 us
    pallas_call x1, Pallas kernels: 45 us -> 44 us  [local(): pl.pallas_call(functools.partial(kernel, nr, nc, tile, rates), out_shape=...]
    pallas_call x1, Pallas kernels: 1.48 us -> 0.65 us  [local(): pl.pallas_call(finish, out_shape=outs, in_specs=[vmem] * 3, out_specs=[vm...]
where the time goes in v1:
time: 45.4 us; the launch traced here: 45.3 us
  Pallas kernels  44.6 us (98%)
  between operations  0.64 us (1%)
    pallas_call x1, Pallas kernels, local(): pl.pallas_call(functools.partial(kernel, nr, nc, tile, rates), out_shape=...  44 us

profile of v1, /device:TPU:0, one launch (start us, length us, event | category | flops | bytes accessed | tf_op | source)
XLA Modules:
  0.0 45.3 jit_solution(11384584509222523384)
XLA Ops:
  0.6 44.0 %shard_map.67 = (f32[64,128]{1,0:T(8,128)S(1)}, f32[128,128]{1,0:T(8,128)S(1)}, f32[16,128]{1,0:T(8,128)S(1)}) custom-call(bf16[512,8192]{1,0:T(8,128)(2,1)} %counts_hbm.1, f32[64,128]{1,0:T(8,128)} %a_hbm.1, f32[128,128]{1,0:T(8,128)} %b_hbm.1, f32[16,128]{1,0:T(8,128)} %c_hbm.1), custom_call_target="tpu_custom_call" | custom-call | tf_op jit(solution)/shard_map/pallas_call | solution.py:243
  44.6 0.6 %shard_map.68 = (f32[64,128]{1,0:T(8,128)}, f32[128,128]{1,0:T(8,128)}, f32[16,128]{1,0:T(8,128)}) custom-call(f32[64,128]{1,0:T(8,128)S(1)} %get-tuple-element.6.a, f32[128,128]{1,0:T(8,128)S(1)} %get-tuple-element.7.b, f32[16,128]{1,0:T(8,128)S(1)} %get-tuple-element.8.c), custom_call_target="tpu_custom_call" | custom-call | tf_op jit(solution)/shard_map/pallas_call | solution.py:277

commit v2 on v1

v2 whole, which is shorter than its diff:
```python
import functools
import math

import jax
import jax.numpy as jnp
from jax import lax
from jax.experimental import pallas as pl
from jax.experimental.pallas import tpu as pltpu
from jax.sharding import PartitionSpec as P

ITERS = 2
LATE = 0
MESH = pl.DeviceIdType.MESH
F32 = jnp.float32
BF16 = jnp.bfloat16


def kernel(nr, nc, tile, rates, counts_hbm, a_hbm, b_hbm, c_hbm, a_out, b_out, c_out,
           a_now, b_now, c_in, in_sem, counts, all_a, all_b, send_a, send_b, recv_a, recv_b, part_c, sum_c,
           held_a, trans_a, acc_a, acc_c, resid, resid_late, scaled, mixed_t, grad_b,
           cnt_sem, ag_send, ag_recv, bg_send, bg_recv, ar_send, ar_recv, br_send, br_recv,
           c1_send, c1_recv, c2_send, c2_recv):
    row, col = lax.axis_index("rows"), lax.axis_index("cols")
    rate_a, rate_b, rate_c = rates
    own_a, rank = a_now.shape
    own_b = b_now.shape[0]
    depth = c_in.shape[0]
    tiles = counts.shape[1]
    per = tiles // nr
    width = tile // depth

    half, quarter = nc // 2, nc // 4
    seat = lax.rem(col + nc - quarter, nc)
    mine, spot = lax.div(seat, half), lax.rem(seat, half)
    col_peers = [lax.rem(seat + off, nc) for off in range(1, nc)]
    row_peers = [lax.rem(row + off, nr) for off in range(1, nr)]
    half_rows = half * own_a
    quarter_rows = quarter * own_a

    def at_col(p):
        return {"cols": lax.rem(p + quarter, nc)}

    def at_row(p):
        return {"rows": p}

    barrier = pltpu.get_barrier_semaphore()
    for p in col_peers:
        pl.semaphore_signal(barrier, inc=1, device_id=at_col(p), device_id_type=MESH)
    for p in row_peers:
        pl.semaphore_signal(barrier, inc=1, device_id=at_row(p), device_id_type=MESH)

    fetches = [pltpu.make_async_copy(src, dst, in_sem.at[n])
               for n, (src, dst) in enumerate(((a_hbm, a_now), (b_hbm, b_now), (c_hbm, c_in)))]
    for fetch in fetches:
        fetch.start()

    def loads(h, t):
        spans = [(quarter_rows, half_rows, 0)] if h == 0 else [(3 * quarter_rows, quarter_rows, 0), (0, quarter_rows, quarter_rows)]
        return [pltpu.make_async_copy(
            counts_hbm.at[pl.ds(first, n), pl.ds(pl.multiple_of(t * tile, tile), tile)],
            counts.at[h, t, pl.ds(to, n)], cnt_sem.at[h + k, t]) for k, (first, n, to) in enumerate(spans)]

    def chunk(side, d):
        return lax.rem(row + side + d, nr)

    for fetch in fetches:
        fetch.wait()
    all_a[0, seat] = a_now[...].astype(BF16)
    all_b[0, row] = b_now[...].astype(BF16)

    pl.semaphore_wait(barrier, nc + nr - 2)

    class Exchange:
        def __init__(self, send, recv, ss, rs, at, me):
            self.args = (send, recv, ss, rs, at, me)

        def to(self, p):
            send, recv, ss, rs, at, me = self.args
            return pltpu.make_async_remote_copy(
                src_ref=recv.at[me] if send is None else send.at[p], dst_ref=recv.at[me],
                send_sem=ss.at[p], recv_sem=rs.at[me], device_id=at(p), device_id_type=MESH)

        def start(self, peers):
            for p in peers:
                self.to(p).start()

        def wait_recv(self, peers):
            send, recv, ss, rs, at, me = self.args
            for p in peers:
                pltpu.make_async_remote_copy(
                    src_ref=recv.at[p], dst_ref=recv.at[p], send_sem=ss.at[p], recv_sem=rs.at[p],
                    device_id=at(p), device_id_type=MESH).wait_recv()

        def wait_send(self, peers):
            for p in peers:
                self.to(p).wait_send()

    def over_half(act, h):
        act([h * half + lax.rem(spot + off, half) for off in range(1, half)])

        @pl.when(mine != h)
        def _():
            act([h * half + spot])

    pending = []
    shared_c = c_in[...]

    def gather(it):
        return (Exchange(None, all_a.at[it], ag_send.at[it], ag_recv.at[it], at_col, seat),
                Exchange(None, all_b.at[it], bg_send.at[it], bg_recv.at[it], at_row, row))

    gather_a, gather_b = gather(0)
    gather_b.start(row_peers)
    gather_a.start(col_peers)
    for h in range(2):
        for d in range(nr):
            for s in range(per):
                for load in loads(h, chunk(h, d) * per + s):
                    load.start()

    late_update = None

    for it in range(ITERS):
        last = it == ITERS - 1
        pending += [(gather_a, col_peers), (gather_b, row_peers)]
        scatter_a = Exchange(send_a.at[it], recv_a.at[it], ar_send.at[it], ar_recv.at[it], at_col, seat)
        scatter_b = Exchange(send_b.at[it], recv_b.at[it], br_send.at[it], br_recv.at[it], at_row, row)
        cols_c = Exchange(None, part_c.at[it], c1_send.at[it], c1_recv.at[it], at_col, seat)
        rows_c = Exchange(None, sum_c.at[it], c2_send.at[it], c2_recv.at[it], at_row, row)
        pending += [(scatter_a, col_peers), (scatter_b, row_peers), (cols_c, col_peers), (rows_c, row_peers)]
        if not last:
            next_a, next_b = gather(it + 1)
        acc_c[...] = jnp.zeros_like(acc_c)

        def send_half(h, it=it, scatter_a=scatter_a):
            for k in range(half):
                send_a[it, h * half + k] = acc_a[h, pl.ds(k * own_a, own_a), :].astype(BF16)
            over_half(scatter_a.start, h)

        def update_a(it=it, last=last, scatter_a=scatter_a, next_a=None if last else next_a):
            scatter_a.wait_recv(col_peers)
            recv_a[it, seat] = jnp.zeros((own_a, rank), BF16)
            total = (acc_a[mine, pl.ds(pl.multiple_of(spot * own_a, own_a), own_a), :]
                     + jnp.sum(recv_a[it].astype(F32), axis=0))
            if last:
                a_out[...] = a_now[...] - rate_a * total
            else:
                a_now[...] = a_now[...] - rate_a * total
                all_a[it + 1, seat] = a_now[...].astype(BF16)
                next_a.start(col_peers)

        for h in range(2):
            over_half(gather_a.wait_recv, h)
            rows_a = all_a[it, pl.ds(h * half, half)].reshape(half_rows, rank)
            held_a[...] = rows_a
            trans_a[...] = rows_a.T
            if h == 0:
                acc_a[0] = jnp.zeros((half_rows, rank), F32)

            def produce(q, s, slot):
                t = q * per + s
                if h == 0:
                    rows_b = all_b[it, q, pl.ds(s * width, width), :].astype(F32)
                    scaled[t] = (rows_b[:, None, :] * shared_c[None, :, :]).astype(BF16).reshape(tile, rank)
                log_rate = lax.dot_general(
                    held_a[...], scaled[t], (((1,), (1,)), ((), ())), preferred_element_type=F32)
                found = (jnp.exp(log_rate) - counts[h, t].astype(F32)).astype(BF16)
                if h == 0:
                    resid[slot] = found
                else:
                    resid_late[t] = found

            def consume(q, s, slot):
                t = q * per + s
                if h == 0:
                    acc_a[0] += jnp.dot(resid[slot], scaled[t], preferred_element_type=F32)
                    mixed_t[t] = jnp.dot(trans_a[...], resid[slot], preferred_element_type=F32)
                    return
                turned = jnp.dot(trans_a[...], resid_late[t], preferred_element_type=F32)
                mixed = (mixed_t[t] + turned).T.reshape(width, depth, rank)
                rows_b = all_b[it, q, pl.ds(s * width, width), :].astype(F32)
                grad_b[pl.ds(s * width, width), :] = jnp.sum(mixed * shared_c[None, :, :], axis=1)
                acc_c[...] += jnp.sum(mixed * rows_b[:, None, :], axis=0)

            def ready(d):
                q = chunk(h, d)
                if it == 0:
                    for s in range(per):
                        for load in loads(h, q * per + s):
                            load.wait()
                return q

            def step(d, carry):
                q, q_next = chunk(h, d), chunk(h, d + 1)
                if h == 0 or it == 0:
                    @pl.when(d < nr - 1)
                    def _():
                        ready(d + 1)
                        if h == 0:
                            gather_b.wait_recv([q_next])
                for s in range(per):
                    if s + 1 < per:
                        produce(q, s + 1, (s + 1) % 2)
                    else:
                        produce(q_next, 0, 0)
                    consume(q, s, s % 2)
                if h == 0 and late_update is not None:
                    @pl.when((d == LATE) & (mine == 1))
                    def _():
                        late_update()
                if h == 1:
                    send_b[it, q] = grad_b[...].astype(BF16)

                    @pl.when(d < nr - 1)
                    def _():
                        scatter_b.start([q])

                return carry

            produce(ready(0), 0, 0)
            lax.fori_loop(0, nr, step, 0)
            if h == 0:
                send_half(0)

        part_c[it, seat] = acc_c[...].astype(BF16)
        cols_c.start(col_peers)

        acc_a[1] = jnp.zeros((half_rows, rank), F32)

        def gather_grad(g, carry):
            total = acc_a[1]
            for s in range(per):
                total += jnp.dot(resid_late[g * per + s], scaled[g * per + s], preferred_element_type=F32)
            acc_a[1] = total
            return carry

        lax.fori_loop(0, nr, gather_grad, 0)
        send_half(1)

        scatter_b.wait_recv(row_peers)
        recv_b[it, row] = jnp.zeros((own_b, rank), BF16)
        b_next = b_now[...] - rate_b * (grad_b[...] + jnp.sum(recv_b[it].astype(F32), axis=0))
        if last:
            b_out[...] = b_next
        else:
            b_now[...] = b_next
            all_b[it + 1, row] = b_next.astype(BF16)
            next_b.start(row_peers)

        @pl.when(mine == 0)
        def _():
            update_a()

        cols_c.wait_recv(col_peers)
        sum_c[it, row] = jnp.sum(part_c[it].astype(F32), axis=0)
        rows_c.start(row_peers)

        if last:
            @pl.when(mine == 1)
            def _():
                update_a()
        late_update = update_a

        rows_c.wait_recv(row_peers)
        shared_c = shared_c - rate_c * jnp.sum(sum_c[it], axis=0)
        if last:
            c_out[...] = shared_c
        else:
            gather_a, gather_b = next_a, next_b

    for group, peers in pending:
        group.wait_send(peers)


def finish(a, b, c, a_out, b_out, c_out):
    a_out[...] = a[...]
    b_out[...] = b[...]
    c_out[...] = c[...]


def local(nr, nc, counts, start_a, start_b, start_c):
    rows_here, flat_width = counts.shape
    own_a, rank = start_a.shape
    own_b = start_b.shape[0]
    depth = start_c.shape[0]
    cols_here = flat_width // depth
    total_i, total_j = rows_here * nr, cols_here * nc
    rates = (0.3 / math.sqrt(total_j * depth), 0.3 / math.sqrt(total_i * depth), 0.3 / math.sqrt(total_i * total_j))
    tile = 512
    tiles = flat_width // tile
    vmem = pl.BlockSpec(memory_space=pltpu.VMEM)
    dma = pltpu.SemaphoreType.DMA
    outs = [jax.ShapeDtypeStruct(x.shape, F32) for x in (start_a, start_b, start_c)]
    half_rows = rows_here // 2
    found = pl.pallas_call(
        functools.partial(kernel, nr, nc, tile, rates),
        out_shape=[pltpu.VMEM(x.shape, F32) for x in (start_a, start_b, start_c)],
        in_specs=[pl.BlockSpec(memory_space=pl.ANY)] * 4,
        out_specs=[vmem] * 3,
        scratch_shapes=[
            pltpu.VMEM(start_a.shape, F32), pltpu.VMEM(start_b.shape, F32), pltpu.VMEM(start_c.shape, F32),
            dma((3,)),
            pltpu.VMEM((2, tiles, half_rows, tile), BF16),
            pltpu.VMEM((ITERS, nc, own_a, rank), BF16),
            pltpu.VMEM((ITERS, nr, own_b, rank), BF16),
            pltpu.VMEM((ITERS, nc, own_a, rank), BF16),
            pltpu.VMEM((ITERS, nr, own_b, rank), BF16),
            pltpu.VMEM((ITERS, nc, own_a, rank), BF16),
            pltpu.VMEM((ITERS, nr, own_b, rank), BF16),
            pltpu.VMEM((ITERS, nc, depth, rank), BF16),
            pltpu.VMEM((ITERS, nr, depth, rank), F32),
            pltpu.VMEM((half_rows, rank), BF16),
            pltpu.VMEM((rank, half_rows), BF16),
            pltpu.VMEM((2, half_rows, rank), F32),
            pltpu.VMEM((depth, rank), F32),
            pltpu.VMEM((2, half_rows, tile), BF16),
            pltpu.VMEM((tiles, half_rows, tile), BF16),
            pltpu.VMEM((tiles, tile, rank), BF16),
            pltpu.VMEM((tiles, rank, tile), F32),
            pltpu.VMEM((own_b, rank), F32),
            dma((3, tiles)),
            dma((ITERS, nc)), dma((ITERS, nc)), dma((ITERS, nr)), dma((ITERS, nr)),
            dma((ITERS, nc)), dma((ITERS, nc)), dma((ITERS, nr)), dma((ITERS, nr)),
            dma((ITERS, nc)), dma((ITERS, nc)), dma((ITERS, nr)), dma((ITERS, nr)),
        ],
        compiler_params=pltpu.CompilerParams(
            collective_id=0, has_side_effects=True, vmem_limit_bytes=56 * 1024 * 1024),
    )(counts, start_a, start_b, start_c)
    held = [pltpu.with_memory_space_constraint(x, pltpu.VMEM) for x in found]
    return pl.pallas_call(finish, out_shape=outs, in_specs=[vmem] * 3, out_specs=[vmem] * 3)(*held)


def solution(mesh):
    nr, nc = mesh.shape["rows"], mesh.shape["cols"]
    placed = (P("rows", "cols"), P(("rows", "cols"), None), P(("cols", "rows"), None), P())
    return jax.shard_map(
        functools.partial(local, nr, nc),
        mesh=mesh,
        in_specs=placed,
        out_specs=(P(("rows", "cols"), None), P(("cols", "rows"), None), P()),
        check_vma=False,
    )
```

time: 45.4 us -> 44.5 us (0.980)
  Pallas kernels: 44.6 us -> 43.7 us
    pallas_call x1, Pallas kernels: 44 us -> 43.1 us  [local(): pl.pallas_call(functools.partial(kernel, nr, nc, tile, rates), out_shape=...]
where the time goes in v2:
time: 44.5 us; the launch traced here: 44.4 us
  Pallas kernels  43.7 us (98%)
  between operations  0.64 us (1%)
    pallas_call x1, Pallas kernels, local(): pl.pallas_call(functools.partial(kernel, nr, nc, tile, rates), out_shape=...  43.1 us

profile of v2, /device:TPU:0, one launch (start us, length us, event | category | flops | bytes accessed | tf_op | source)
XLA Modules:
  0.0 44.4 jit_solution(8494468845774638200)
XLA Ops:
  0.6 43.1 %shard_map.67 = (f32[64,128]{1,0:T(8,128)S(1)}, f32[128,128]{1,0:T(8,128)S(1)}, f32[16,128]{1,0:T(8,128)S(1)}) custom-call(bf16[512,8192]{1,0:T(8,128)(2,1)} %counts_hbm.1, f32[64,128]{1,0:T(8,128)} %a_hbm.1, f32[128,128]{1,0:T(8,128)} %b_hbm.1, f32[16,128]{1,0:T(8,128)} %c_hbm.1), custom_call_target="tpu_custom_call" | custom-call | tf_op jit(solution)/shard_map/pallas_call | solution.py:295
  43.7 0.6 %shard_map.68 = (f32[64,128]{1,0:T(8,128)}, f32[128,128]{1,0:T(8,128)}, f32[16,128]{1,0:T(8,128)}) custom-call(f32[64,128]{1,0:T(8,128)S(1)} %get-tuple-element.6.a, f32[128,128]{1,0:T(8,128)S(1)} %get-tuple-element.7.b, f32[16,128]{1,0:T(8,128)S(1)} %get-tuple-element.8.c), custom_call_target="tpu_custom_call" | custom-call | tf_op jit(solution)/shard_map/pallas_call | solution.py:330

commit v3 on v2

--- a/solution.py
+++ b/solution.py
@@ -9,7 +9,6 @@
 from jax.sharding import PartitionSpec as P
 
 ITERS = 2
-LATE = 0
 MESH = pl.DeviceIdType.MESH
 F32 = jnp.float32
 BF16 = jnp.bfloat16
@@ -17,7 +16,7 @@
 
 def kernel(nr, nc, tile, rates, counts_hbm, a_hbm, b_hbm, c_hbm, a_out, b_out, c_out,
            a_now, b_now, c_in, in_sem, counts, all_a, all_b, send_a, send_b, recv_a, recv_b, part_c, sum_c,
-           held_a, trans_a, acc_a, acc_c, resid, resid_late, scaled, mixed_t, grad_b,
+           held_a, trans_a, acc_a, acc_c, resid, scaled, mixed_t, grad_b,
            cnt_sem, ag_send, ag_recv, bg_send, bg_recv, ar_send, ar_recv, br_send, br_recv,
            c1_send, c1_recv, c2_send, c2_recv):
     row, col = lax.axis_index("rows"), lax.axis_index("cols")
@@ -25,8 +24,9 @@
     own_a, rank = a_now.shape
     own_b = b_now.shape[0]
     depth = c_in.shape[0]
-    tiles = counts.shape[1]
+    tiles = scaled.shape[0]
     per = tiles // nr
+    span = per * tile
     width = tile // depth
 
     half, quarter = nc // 2, nc // 4
@@ -54,11 +54,11 @@
     for fetch in fetches:
         fetch.start()
 
-    def loads(h, t):
+    def loads(h, q):
         spans = [(quarter_rows, half_rows, 0)] if h == 0 else [(3 * quarter_rows, quarter_rows, 0), (0, quarter_rows, quarter_rows)]
         return [pltpu.make_async_copy(
-            counts_hbm.at[pl.ds(first, n), pl.ds(pl.multiple_of(t * tile, tile), tile)],
-            counts.at[h, t, pl.ds(to, n)], cnt_sem.at[h + k, t]) for k, (first, n, to) in enumerate(spans)]
+            counts_hbm.at[pl.ds(first, n), pl.ds(pl.multiple_of(q * span, span), span)],
+            counts.at[h, q, pl.ds(to, n)], cnt_sem.at[h + k, q]) for k, (first, n, to) in enumerate(spans)]
 
     def chunk(side, d):
         return lax.rem(row + side + d, nr)
@@ -71,29 +71,35 @@
     pl.semaphore_wait(barrier, nc + nr - 2)
 
     class Exchange:
-        def __init__(self, send, recv, ss, rs, at, me):
+        def __init__(self, send, recv, ss, rs, at, me, group):
             self.args = (send, recv, ss, rs, at, me)
+            self.group = group
 
         def to(self, p):
             send, recv, ss, rs, at, me = self.args
             return pltpu.make_async_remote_copy(
                 src_ref=recv.at[me] if send is None else send.at[p], dst_ref=recv.at[me],
-                send_sem=ss.at[p], recv_sem=rs.at[me], device_id=at(p), device_id_type=MESH)
+                send_sem=ss, recv_sem=self.seat_sem(me), device_id=at(p), device_id_type=MESH)
 
         def start(self, peers):
             for p in peers:
                 self.to(p).start()
 
-        def wait_recv(self, peers):
+        def seat_sem(self, p):
+            rs, group = self.args[3], self.group
+            return rs.at[lax.div(p, group)]
+
+        def bytes_of(self, n, p):
             send, recv, ss, rs, at, me = self.args
-            for p in peers:
-                pltpu.make_async_remote_copy(
-                    src_ref=recv.at[p], dst_ref=recv.at[p], send_sem=ss.at[p], recv_sem=rs.at[p],
-                    device_id=at(p), device_id_type=MESH).wait_recv()
-
-        def wait_send(self, peers):
-            for p in peers:
-                self.to(p).wait_send()
+            return pltpu.make_async_remote_copy(
+                src_ref=recv.at[pl.ds(0, n)], dst_ref=recv.at[pl.ds(0, n)], send_sem=ss, recv_sem=self.seat_sem(p),
+                device_id=at(lax.rem(me + 1, recv.shape[0])), device_id_type=MESH)
+
+        def wait_recv(self, n, p):
+            self.bytes_of(n, p).wait_recv()
+
+        def wait_send(self):
+            self.bytes_of(self.args[1].shape[0] - 1, self.args[5]).wait_send()
 
     def over_half(act, h):
         act([h * half + lax.rem(spot + off, half) for off in range(1, half)])
@@ -106,28 +112,25 @@
     shared_c = c_in[...]
 
     def gather(it):
-        return (Exchange(None, all_a.at[it], ag_send.at[it], ag_recv.at[it], at_col, seat),
-                Exchange(None, all_b.at[it], bg_send.at[it], bg_recv.at[it], at_row, row))
+        return (Exchange(None, all_a.at[it], ag_send.at[it], ag_recv.at[it], at_col, seat, half),
+                Exchange(None, all_b.at[it], bg_send.at[it], bg_recv.at[it], at_row, row, 1))
 
     gather_a, gather_b = gather(0)
     gather_b.start(row_peers)
     gather_a.start(col_peers)
     for h in range(2):
         for d in range(nr):
-            for s in range(per):
-                for load in loads(h, chunk(h, d) * per + s):
-                    load.start()
-
-    late_update = None
+            for load in loads(h, chunk(h, d)):
+                load.start()
 
     for it in range(ITERS):
         last = it == ITERS - 1
-        pending += [(gather_a, col_peers), (gather_b, row_peers)]
-        scatter_a = Exchange(send_a.at[it], recv_a.at[it], ar_send.at[it], ar_recv.at[it], at_col, seat)
-        scatter_b = Exchange(send_b.at[it], recv_b.at[it], br_send.at[it], br_recv.at[it], at_row, row)
-        cols_c = Exchange(None, part_c.at[it], c1_send.at[it], c1_recv.at[it], at_col, seat)
-        rows_c = Exchange(None, sum_c.at[it], c2_send.at[it], c2_recv.at[it], at_row, row)
-        pending += [(scatter_a, col_peers), (scatter_b, row_peers), (cols_c, col_peers), (rows_c, row_peers)]
+        pending += [gather_a, gather_b]
+        scatter_a = Exchange(send_a.at[it], recv_a.at[it], ar_send.at[it], ar_recv.at[it], at_col, seat, nc)
+        scatter_b = Exchange(send_b.at[it], recv_b.at[it], br_send.at[it], br_recv.at[it], at_row, row, nr)
+        cols_c = Exchange(None, part_c.at[it], c1_send.at[it], c1_recv.at[it], at_col, seat, nc)
+        rows_c = Exchange(None, sum_c.at[it], c2_send.at[it], c2_recv.at[it], at_row, row, nr)
+        pending += [scatter_a, scatter_b, cols_c, rows_c]
         if not last:
             next_a, next_b = gather(it + 1)
         acc_c[...] = jnp.zeros_like(acc_c)
@@ -138,7 +141,7 @@
             over_half(scatter_a.start, h)
 
         def update_a(it=it, last=last, scatter_a=scatter_a, next_a=None if last else next_a):
-            scatter_a.wait_recv(col_peers)
+            scatter_a.wait_recv(nc - 1, 0)
             recv_a[it, seat] = jnp.zeros((own_a, rank), BF16)
             total = (acc_a[mine, pl.ds(pl.multiple_of(spot * own_a, own_a), own_a), :]
                      + jnp.sum(recv_a[it].astype(F32), axis=0))
@@ -150,12 +153,18 @@
                 next_a.start(col_peers)
 
         for h in range(2):
-            over_half(gather_a.wait_recv, h)
+            @pl.when(mine == h)
+            def _():
+                gather_a.wait_recv(half - 1, h * half)
+
+            @pl.when(mine != h)
+            def _():
+                gather_a.wait_recv(half, h * half)
+
             rows_a = all_a[it, pl.ds(h * half, half)].reshape(half_rows, rank)
             held_a[...] = rows_a
             trans_a[...] = rows_a.T
-            if h == 0:
-                acc_a[0] = jnp.zeros((half_rows, rank), F32)
+            acc_a[h] = jnp.zeros((half_rows, rank), F32)
 
             def produce(q, s, slot):
                 t = q * per + s
@@ -164,19 +173,15 @@
                     scaled[t] = (rows_b[:, None, :] * shared_c[None, :, :]).astype(BF16).reshape(tile, rank)
                 log_rate = lax.dot_general(
                     held_a[...], scaled[t], (((1,), (1,)), ((), ())), preferred_element_type=F32)
-                found = (jnp.exp(log_rate) - counts[h, t].astype(F32)).astype(BF16)
-                if h == 0:
-                    resid[slot] = found
-                else:
-                    resid_late[t] = found
+                resid[slot] = (jnp.exp(log_rate) - counts[h, q, :, pl.ds(s * tile, tile)].astype(F32)).astype(BF16)
 
             def consume(q, s, slot):
                 t = q * per + s
+                acc_a[h] += jnp.dot(resid[slot], scaled[t], preferred_element_type=F32)
+                turned = jnp.dot(trans_a[...], resid[slot], preferred_element_type=F32)
                 if h == 0:
-                    acc_a[0] += jnp.dot(resid[slot], scaled[t], preferred_element_type=F32)
-                    mixed_t[t] = jnp.dot(trans_a[...], resid[slot], preferred_element_type=F32)
+                    mixed_t[t] = turned
                     return
-                turned = jnp.dot(trans_a[...], resid_late[t], preferred_element_type=F32)
                 mixed = (mixed_t[t] + turned).T.reshape(width, depth, rank)
                 rows_b = all_b[it, q, pl.ds(s * width, width), :].astype(F32)
                 grad_b[pl.ds(s * width, width), :] = jnp.sum(mixed * shared_c[None, :, :], axis=1)
@@ -185,9 +190,8 @@
             def ready(d):
                 q = chunk(h, d)
                 if it == 0:
-                    for s in range(per):
-                        for load in loads(h, q * per + s):
-                            load.wait()
+                    for load in loads(h, q):
+                        load.wait()
                 return q
 
             def step(d, carry):
@@ -197,17 +201,13 @@
                     def _():
                         ready(d + 1)
                         if h == 0:
-                            gather_b.wait_recv([q_next])
+                            gather_b.wait_recv(1, q_next)
                 for s in range(per):
                     if s + 1 < per:
                         produce(q, s + 1, (s + 1) % 2)
                     else:
                         produce(q_next, 0, 0)
                     consume(q, s, s % 2)
-                if h == 0 and late_update is not None:
-                    @pl.when((d == LATE) & (mine == 1))
-                    def _():
-                        late_update()
                 if h == 1:
                     send_b[it, q] = grad_b[...].astype(BF16)
 
@@ -225,19 +225,9 @@
         part_c[it, seat] = acc_c[...].astype(BF16)
         cols_c.start(col_peers)
 
-        acc_a[1] = jnp.zeros((half_rows, rank), F32)
-
-        def gather_grad(g, carry):
-            total = acc_a[1]
-            for s in range(per):
-                total += jnp.dot(resid_late[g * per + s], scaled[g * per + s], preferred_element_type=F32)
-            acc_a[1] = total
-            return carry
-
-        lax.fori_loop(0, nr, gather_grad, 0)
         send_half(1)
 
-        scatter_b.wait_recv(row_peers)
+        scatter_b.wait_recv(nr - 1, 0)
         recv_b[it, row] = jnp.zeros((own_b, rank), BF16)
         b_next = b_now[...] - rate_b * (grad_b[...] + jnp.sum(recv_b[it].astype(F32), axis=0))
         if last:
@@ -251,7 +241,7 @@
         def _():
             update_a()
 
-        cols_c.wait_recv(col_peers)
+        cols_c.wait_recv(nc - 1, 0)
         sum_c[it, row] = jnp.sum(part_c[it].astype(F32), axis=0)
         rows_c.start(row_peers)
 
@@ -259,17 +249,18 @@
             @pl.when(mine == 1)
             def _():
                 update_a()
-        late_update = update_a
-
-        rows_c.wait_recv(row_peers)
+        rows_c.wait_recv(nr - 1, 0)
         shared_c = shared_c - rate_c * jnp.sum(sum_c[it], axis=0)
         if last:
             c_out[...] = shared_c
         else:
+            @pl.when(mine == 1)
+            def _():
+                update_a()
             gather_a, gather_b = next_a, next_b
 
-    for group, peers in pending:
-        group.wait_send(peers)
+    for group in pending:
+        group.wait_send()
 
 
 def finish(a, b, c, a_out, b_out, c_out):
@@ -300,7 +291,7 @@
         scratch_shapes=[
             pltpu.VMEM(start_a.shape, F32), pltpu.VMEM(start_b.shape, F32), pltpu.VMEM(start_c.shape, F32),
             dma((3,)),
-            pltpu.VMEM((2, tiles, half_rows, tile), BF16),
+            pltpu.VMEM((2, nr, half_rows, flat_width // nr), BF16),
             pltpu.VMEM((ITERS, nc, own_a, rank), BF16),
             pltpu.VMEM((ITERS, nr, own_b, rank), BF16),
             pltpu.VMEM((ITERS, nc, own_a, rank), BF16),
@@ -314,14 +305,13 @@
             pltpu.VMEM((2, half_rows, rank), F32),
             pltpu.VMEM((depth, rank), F32),
             pltpu.VMEM((2, half_rows, tile), BF16),
-            pltpu.VMEM((tiles, half_rows, tile), BF16),
             pltpu.VMEM((tiles, tile, rank), BF16),
             pltpu.VMEM((tiles, rank, tile), F32),
             pltpu.VMEM((own_b, rank), F32),
-            dma((3, tiles)),
-            dma((ITERS, nc)), dma((ITERS, nc)), dma((ITERS, nr)), dma((ITERS, nr)),
-            dma((ITERS, nc)), dma((ITERS, nc)), dma((ITERS, nr)), dma((ITERS, nr)),
-            dma((ITERS, nc)), dma((ITERS, nc)), dma((ITERS, nr)), dma((ITERS, nr)),
+            dma((3, nr)),
+            dma((ITERS,)), dma((ITERS, 2)), dma((ITERS,)), dma((ITERS, nr)),
+            dma((ITERS,)), dma((ITERS, 1)), dma((ITERS,)), dma((ITERS, 1)),
+            dma((ITERS,)), dma((ITERS, 1)), dma((ITERS,)), dma((ITERS, 1)),
         ],
         compiler_params=pltpu.CompilerParams(
             collective_id=0, has_side_effects=True, vmem_limit_bytes=56 * 1024 * 1024),

time: 44.5 us -> 42.5 us (0.955)
  Pallas kernels: 43.7 us -> 41.7 us
    pallas_call x1, Pallas kernels: 43.1 us -> 41.1 us  [local(): pl.pallas_call(functools.partial(kernel, nr, nc, tile, rates), out_shape=...]
where the time goes in v3:
time: 42.5 us; the launch traced here: 42.3 us
  Pallas kernels  41.7 us (98%)
  between operations  0.64 us (2%)
    pallas_call x1, Pallas kernels, local(): pl.pallas_call(functools.partial(kernel, nr, nc, tile, rates), out_shape=...  41.1 us

profile of v3, /device:TPU:0, one launch (start us, length us, event | category | flops | bytes accessed | tf_op | source)
XLA Modules:
  0.0 42.3 jit_solution(12047512628228140731)
XLA Ops:
  0.6 41.1 %shard_map.67 = (f32[64,128]{1,0:T(8,128)S(1)}, f32[128,128]{1,0:T(8,128)S(1)}, f32[16,128]{1,0:T(8,128)S(1)}) custom-call(bf16[512,8192]{1,0:T(8,128)(2,1)} %counts_hbm.1, f32[64,128]{1,0:T(8,128)} %a_hbm.1, f32[128,128]{1,0:T(8,128)} %b_hbm.1, f32[16,128]{1,0:T(8,128)} %c_hbm.1), custom_call_target="tpu_custom_call" | custom-call | tf_op jit(solution)/shard_map/pallas_call | solution.py:286
  41.7 0.6 %shard_map.68 = (f32[64,128]{1,0:T(8,128)}, f32[128,128]{1,0:T(8,128)}, f32[16,128]{1,0:T(8,128)}) custom-call(f32[64,128]{1,0:T(8,128)S(1)} %get-tuple-element.6.a, f32[128,128]{1,0:T(8,128)S(1)} %get-tuple-element.7.b, f32[16,128]{1,0:T(8,128)S(1)} %get-tuple-element.8.c), custom_call_target="tpu_custom_call" | custom-call | tf_op jit(solution)/shard_map/pallas_call | solution.py:320
